TPU v7x, 512 devices: a whole 4x8x8 slice. The times are simulated.
512 devices in a mesh: row: 16 (over z_hi, x, core), col: 32 (over y, z_lo).
Axes of the slice: x: 4, y: 8, z: 8 (z_hi: 2, z_lo: 4; z = z_hi * 4 + z_lo), core: 2. Of those that a mesh axis runs over, the one named last changes fastest.
Arguments:
- trunk: bfloat16 [4096, 512], P('row', 'col'), may hold values from -6 to 6
- proj_weight: bfloat16 [512, 128], P('col'), may hold values from -0.25 to 0.25
- conv_kernel: bfloat16 [9, 64, 64], replicated, may hold values from -0.25 to 0.25
- norm_gain: float32 [64], replicated, may hold values from 0.1 to 1.9
- norm_bias: float32 [64], replicated, may hold values from -3 to 3
Outputs:
- contact_map: bfloat16 [4096, 64, 4096], P('row', None, 'col')
All inputs are finite; a program needn't handle non-finite values.
Results may differ from a plain program's by a relative error of at most 0.0095.
Values may be sent and summed in bfloat16 or wider, within the bound.
No kernel may reach another device: no remote copies, remote signals or barrier semaphores. Data moves between devices by JAX's collectives and lax.ppermute only.
A program may use at most 128 MiB of HBM per device.

v0:
```python
import jax
import jax.numpy as jnp
from jax import lax
from jax.sharding import PartitionSpec as P

CONV_DILATION = 4


def pair_features(rows, cols, width):
    row_u = rows[:, :width].astype(jnp.float32)
    row_v = rows[:, width:].astype(jnp.float32)
    col_u = cols[:, :width].astype(jnp.float32).T
    col_v = cols[:, width:].astype(jnp.float32).T
    pair_block = row_u[:, :, None] * col_u[None] + row_v[:, :, None] + col_v[None]
    return pair_block.astype(jnp.bfloat16)


def inside_mask(first_entry, count_total, total_bins):
    position_index = (
        first_entry - CONV_DILATION + jnp.arange(count_total + 2 * CONV_DILATION, dtype=jnp.int32)
    )
    return ((position_index >= 0) & (position_index < total_bins)).astype(jnp.bfloat16)


def symmetric_conv(active, conv_kernel):
    width = conv_kernel.shape[1]
    grid = conv_kernel.reshape(3, 3, width, width).transpose(2, 3, 0, 1)
    stacked = jnp.concatenate([grid, grid.transpose(0, 1, 3, 2)], 0)
    result = lax.conv_general_dilated(
        active[None],
        stacked,
        (1, 1),
        "VALID",
        rhs_dilation=(CONV_DILATION, CONV_DILATION),
        dimension_numbers=("NHCW", "OIHW", "NHCW"),
        preferred_element_type=jnp.float32,
    )[0]
    return 0.5 * (result[:, :width] + result[:, width:])


def per_device(trunk, proj_weight, conv_kernel, norm_gain, norm_bias):
    block_rows = trunk.shape[0]
    width = norm_gain.shape[0]
    total_bins = block_rows * lax.axis_size("row")
    block_columns = total_bins // lax.axis_size("col")
    row_begin = lax.axis_index("row") * block_rows
    column_begin = lax.axis_index("col") * block_columns
    partial_sum = jnp.dot(trunk, proj_weight, preferred_element_type=jnp.float32)
    summed = lax.psum(partial_sum, "col").astype(jnp.bfloat16)
    feature_rows = lax.all_gather(summed, "row", axis=0, tiled=True)
    padded_map = jnp.pad(feature_rows, ((CONV_DILATION, CONV_DILATION), (0, 0)))
    widened_rows = lax.dynamic_slice_in_dim(
        padded_map, row_begin, block_rows + 2 * CONV_DILATION, 0
    )
    widened_columns = lax.dynamic_slice_in_dim(
        padded_map, column_begin, block_columns + 2 * CONV_DILATION, 0
    )
    row_keep = inside_mask(row_begin, block_rows, total_bins)
    col_keep = inside_mask(column_begin, block_columns, total_bins)
    widened_pair = (
        pair_features(widened_rows, widened_columns, width)
        * row_keep[:, None, None]
        * col_keep[None, None, :]
    )
    active = jnp.maximum(widened_pair, jnp.zeros((), jnp.bfloat16))
    base_offset = widened_pair[
        CONV_DILATION : CONV_DILATION + block_rows, :, CONV_DILATION : CONV_DILATION + block_columns
    ]
    half_sum = symmetric_conv(active, conv_kernel)
    result = (
        base_offset.astype(jnp.float32)
        + norm_gain[None, :, None] * half_sum
        + norm_bias[None, :, None]
    )
    return result.astype(jnp.bfloat16)


def solution(mesh):
    in_specs = (P("row", "col"), P("col", None), P(), P(), P())
    out_specs = P("row", None, "col")
    return jax.shard_map(
        per_device, mesh=mesh, in_specs=in_specs, out_specs=out_specs, check_vma=False
    )
```

profile of v0, /device:TPU:1, one launch (start us, length us, event | category | flops | bytes accessed | tf_op | source)
XLA Modules:
  0.0 331.6 jit_solution(3806741830517226296)
XLA Ops:
  6.5 0.0 copy-start
  6.5 0.0 all-gather.2.cloned.1.call-start
  6.5 0.7 copy-done
  7.2 0.9 fusion.32
  8.1 129.6 %all-reduce.2 = bf16[256,128]{1,0:T(8,128)(2,1)} all-reduce(f32[256,128]{1,0:T(8,128)S(1)} %fusion.32), channel_id=1, replica_groups=mesh['row'=16,'col'=32] {'col'}, use_global_device_ids=true, to_apply=%region_0.0 | all-reduce | flops 32768 | bytes 196608 | tf_op jit(solution)/shard_map/psum | solution.py:49
  137.7 0.0 all-gather.2.cloned.1.call-update
  137.7 1.0 copy.16
  138.8 1.1 copy.15
  139.8 0.1 slice.34
  139.9 0.1 slice.35
  140.0 0.7 broadcast_multiply_fusion
  140.6 86.0 %all-gather.2.cloned.1.call-done = bf16[4096,128]{1,0:T(8,128)(2,1)} async-done(((bf16[256,128]{1,0:T(8,128)(2,1)}), bf16[4096,128]{1,0:T(8,128)(2,1)}) %all-gather.2.cloned.1.call-update) | async-done | bytes 1048592 | tf_op jit(solution)/shard_map/all_gather | solution.py:50
  226.6 1.1 fusion.23
  227.7 0.1 copy.11
  227.8 0.1 copy.12
  228.0 0.9 convert_bitcast_fusion.1
  228.9 5.7 %fusion.19 = bf16[1,264,64,136]{1,2,3,0:T(8,128)(2,1)} fusion(f32[64,136]{0,1:T(8,128)S(1)} %get-tuple-element.8, f32[264,64]{0,1:T(8,128)S(1)} %copy.12, f32[64,136]{0,1:T(8,128)S(1)} %get-tuple-element.7, f32[264,64]{0,1:T(8,128)S(1)} %copy.11, bf16[136]{0:T(256)(128)(2,1)S(1)} %and_convert_fusion, bf16[264]{0:T(512)(128)(2,1)S(1)} %fusion.28), kind=kLoop, calls=%fused_computation.22 | loop fusion | flops 16084992 | bytes 4801312 | tf_op jit(solution)/shard_map/max | solution.py:65
  234.7 0.0 copy-start.3
  234.7 22.0 %copy.14 = bf16[264,64,1,8,17]{1,3,4,0,2:T(8,128)(2,1)} copy(bf16[264,64,1,8,17]{0,1,4,3,2:T(8,128)(2,1)} %bitcast.21) | data formatting | bytes 9191424 | tf_op jit(solution)/shard_map/conv_general_dilated | solution.py:29
  256.7 5.6 %slice.36 = bf16[264,64,1,7,8]{1,3,4,0,2:T(8,128)(2,1)} slice(bf16[264,64,1,8,17]{1,3,4,0,2:T(8,128)(2,1)} %copy.14), slice={[0:264], [0:64], [0:1], [1:8], [0:8]} | slice | bytes 3784704 | tf_op jit(solution)/shard_map/conv_general_dilated | solution.py:29
  262.3 0.0 copy-done.3
  262.3 19.8 %broadcast_select_fusion = f32[256,8,17,128]{3,1,2,0:T(8,128)} fusion(pred[8,17]{0,1:T(8,128)(4,1)S(1)} %copy-done.3, bf16[264,64,1,7,8]{1,3,4,0,2:T(8,128)(2,1)} %slice.36, bf16[264,64,1,8,17]{1,3,4,0,2:T(8,128)(2,1)} %copy.14, bf16[64,64,3,3]{0,1,3,2:T(8,128)(2,1)S(1)} %bitcast.24, bf16[64,64,3,3]{0,1,3,2:T(8,128)(2,1)S(1)} %bitcast.25), kind=kOutput, calls=%fused_computation.16 | convolution fusion | flops 5158854656 | bytes 24461448 | tf_op jit(solution)/shard_map/conv_general_dilated | solution.py:29
  282.1 14.9 %copy.17 = f32[256,8,17,128]{3,0,2,1:T(8,128)} copy(f32[256,8,17,128]{3,1,2,0:T(8,128)} %broadcast_select_fusion) | data formatting | bytes 35651584 | tf_op jit(solution)/shard_map/conv_general_dilated | solution.py:29
  297.0 0.0 copy-start.2
  297.0 6.9 %slice_bitcast_fusion = f32[256,128,128]{1,0,2:T(8,128)S(1)} fusion(f32[256,1,136,128]{3,0,2,1:T(8,128)} %bitcast.20), kind=kLoop, calls=%fused_computation.7 | loop fusion | bytes 33554432 | tf_op jit(solution)/shard_map/squeeze | solution.py:29
  303.9 0.0 copy-done.2
  303.9 0.0 copy-start.1
  303.9 9.2 %fusion.4 = bf16[256,64,128]{1,0,2:T(8,128)(2,1)} fusion(f32[256,128,128]{1,0,2:T(8,128)S(1)} %slice_bitcast_fusion, f32[64,128]{0,1:T(8,128)S(1)} %slice.33, f32[256,64]{1,0:T(8,128)S(1)} %slice.32, f32[64,128]{0,1:T(8,128)S(1)} %slice.31, f32[256,64]{1,0:T(8,128)S(1)} %slice.30, f32[64]{0:T(128)S(1)} %copy-done.2, f32[64]{0:T(128)S(1)} %broadcast_multiply_fusion, ...), kind=kLoop, calls=%fused_computation.6 | loop fusion | flops 25165824 | bytes 21169408 | tf_op jit(solution)/shard_map/convert_element_type | solution.py:75
  313.2 11.5 %copy.18 = bf16[256,64,128]{2,1,0:T(8,128)(2,1)} copy(bf16[256,64,128]{1,0,2:T(8,128)(2,1)} %fusion.4) | data formatting | bytes 8388608 | tf_op jit(solution)/shard_map/convert_element_type | solution.py:75
  324.7 0.0 copy-done.1
  (6 shorter events, 0.1 us)
Async XLA Ops:
  6.5 0.7 copy-start
  6.5 220.1 %all-gather.2.cloned.1.call-start = ((), (), s32[]{:S(2)}) async-start(), calls=%async_computation | async-start | bytes 1114112 | tf_op jit(solution)/shard_map/all_gather | solution.py:50
  234.7 27.7 %copy-start.3 = (pred[8,17]{0,1:T(8,128)(4,1)S(1)}, pred[8,17]{0,1:T(8,128)(4,1)}, u32[]{:S(2)}) copy-start(pred[8,17]{0,1:T(8,128)(4,1)} %constant.38) | copy-start | bytes 412
  297.0 6.9 %copy-start.2 = (f32[64]{0:T(128)S(1)}, f32[64]{0:T(128)}, u32[]{:S(2)}) copy-start(f32[64]{0:T(128)} %param.9) | copy-start | bytes 772
  303.9 20.8 %copy-start.1 = (bf16[256,16]{0,1:T(8,128)(2,1)S(1)}, bf16[256,16]{0,1:T(8,128)(2,1)}, u32[]{:S(2)}) copy-start(bf16[256,16]{0,1:T(8,128)(2,1)} %param.5) | copy-start | bytes 24580
Sparse Core Ops, SparseCore 0:
  137.8 88.7 all-gather.1
where the time goes:
time: 332 us
  blocking collectives  130 us (39%)
  waiting for transfers between devices  86 us (26%)
  local copies, waits for them, and re-layouts  64.2 us (19%)
  matrix products  20.6 us (6%)
  other arithmetic  17.7 us (5%)
  between operations  13.5 us (4%)
    psum x1, blocking collectives, per_device(): summed = lax.psum(partial_sum, 'col').astype(jnp.bfloat16)  130 us
    all_gather x1, waiting for transfers between devices, per_device(): feature_rows = lax.all_gather(summed, 'row', axis=0, tiled=True)  86 us
    conv_general_dilated x3, local copies, waits for them, and re-layouts, symmetric_conv(): lax.conv_general_dilated(active[None], stacked, (1, 1), 'VALID', rhs_dila...  42.5 us
    conv_general_dilated x1, matrix products, symmetric_conv(): lax.conv_general_dilated(active[None], stacked, (1, 1), 'VALID', rhs_dila...  19.8 us
    convert_element_type x1, local copies, waits for them, and re-layouts, per_device(): return result.astype(jnp.bfloat16)  11.5 us
    convert_element_type x1, other arithmetic, per_device(): return result.astype(jnp.bfloat16)  9.23 us
    squeeze x1, local copies, waits for them, and re-layouts, symmetric_conv(): lax.conv_general_dilated(active[None], stacked, (1, 1), 'VALID', rhs_dila...  6.93 us
  transfers between devices with their start and end apart: 1, of which 1 were waited for; matrix products, arithmetic and copies ran while one was open for 1% of the time, Pallas kernels for 0%

commit v1 on v0

--- a/solution.py
+++ b/solution.py
@@ -46,7 +46,7 @@
     row_begin = lax.axis_index("row") * block_rows
     column_begin = lax.axis_index("col") * block_columns
     partial_sum = jnp.dot(trunk, proj_weight, preferred_element_type=jnp.float32)
-    summed = lax.psum(partial_sum, "col").astype(jnp.bfloat16)
+    summed = jax.lax.all_gather(partial_sum, "col").sum(axis=0).astype(jnp.bfloat16)
     feature_rows = lax.all_gather(summed, "row", axis=0, tiled=True)
     padded_map = jnp.pad(feature_rows, ((CONV_DILATION, CONV_DILATION), (0, 0)))
     widened_rows = lax.dynamic_slice_in_dim(

time: 332 us -> 347 us (1.045)
  waiting for transfers between devices: 86 us -> 226 us
  blocking collectives: 130 us -> 0 us
    all_gather x0 -> x1, waiting for transfers between devices: none -> 145 us  [per_device(): jax.lax.all_gather(partial_sum, 'col').sum(axis=0).astype(jnp.bfloat16)]
    psum x1 -> x0, blocking collectives: 130 us -> none  [per_device(): summed = lax.psum(partial_sum, 'col').astype(jnp.bfloat16)]
    all_gather x1, waiting for transfers between devices: 86 us -> 80.9 us  [per_device(): feature_rows = lax.all_gather(summed, 'row', axis=0, tiled=True)]
  transfers between devices with their start and end apart: 1 -> 2, of which waited for: 1 -> 2; matrix products, arithmetic and copies ran while one was open for 1% -> 1% of each run, Pallas kernels for 0% -> 0%
where the time goes in v1:
time: 347 us; the launch traced here: 346 us
  waiting for transfers between devices  226 us (65%)
  local copies, waits for them, and re-layouts  64.2 us (19%)
  matrix products  21.3 us (6%)
  other arithmetic  20.7 us (6%)
  between operations  13.5 us (4%)
    all_gather x1, waiting for transfers between devices, per_device(): jax.lax.all_gather(partial_sum, 'col').sum(axis=0).astype(jnp.bfloat16)  145 us
    all_gather x1, waiting for transfers between devices, per_device(): feature_rows = lax.all_gather(summed, 'row', axis=0, tiled=True)  80.9 us
    conv_general_dilated x3, local copies, waits for them, and re-layouts, symmetric_conv(): lax.conv_general_dilated(active[None], stacked, (1, 1), 'VALID', rhs_dila...  42.5 us
    conv_general_dilated x1, matrix products, symmetric_conv(): lax.conv_general_dilated(active[None], stacked, (1, 1), 'VALID', rhs_dila...  19.7 us
    convert_element_type x1, local copies, waits for them, and re-layouts, per_device(): return result.astype(jnp.bfloat16)  11.5 us
    convert_element_type x1, other arithmetic, per_device(): return result.astype(jnp.bfloat16)  9.23 us
  transfers between devices with their start and end apart: 2, of which 2 were waited for; matrix products, arithmetic and copies ran while one was open for 1% of the time, Pallas kernels for 0%

profile of v1, /device:TPU:1, one launch (start us, length us, event | category | flops | bytes accessed | tf_op | source)
XLA Modules:
  0.0 345.9 jit_solution(15805873476978365967)
XLA Ops:
  6.5 0.0 copy-start
  6.5 0.0 all-gather.6.cloned.1.call-start
  6.5 0.7 copy-done
  7.2 1.5 fusion.32
  8.8 0.0 all-gather.6.cloned.1.call-update
  8.8 0.0 all-gather.4.cloned.1.call-start
  8.9 145.2 %all-gather.6.cloned.1.call-done = f32[8192,128]{1,0:T(8,128)} async-done(((f32[256,128]{1,0:T(8,128)}), f32[8192,128]{1,0:T(8,128)}) %all-gather.6.cloned.1.call-update) | async-done | bytes 4194320 | tf_op jit(solution)/shard_map/all_gather | solution.py:49
  154.1 3.0 reduce_sum.9
  157.1 0.0 all-gather.4.cloned.1.call-update
  157.1 1.0 copy.16
  158.2 1.1 copy.15
  159.2 0.1 slice.34
  159.3 0.1 slice.35
  159.4 0.7 broadcast_multiply_fusion
  160.1 80.9 %all-gather.4.cloned.1.call-done = bf16[4096,128]{1,0:T(8,128)(2,1)} async-done(((bf16[256,128]{1,0:T(8,128)(2,1)}), bf16[4096,128]{1,0:T(8,128)(2,1)}) %all-gather.4.cloned.1.call-update) | async-done | bytes 1048592 | tf_op jit(solution)/shard_map/all_gather | solution.py:50
  241.0 1.1 fusion.23
  242.0 0.1 copy.11
  242.2 0.1 copy.12
  242.3 0.9 convert_bitcast_fusion.1
  243.3 5.8 %fusion.19 = bf16[1,264,64,136]{1,2,3,0:T(8,128)(2,1)} fusion(f32[64,136]{0,1:T(8,128)S(1)} %get-tuple-element.8, f32[264,64]{0,1:T(8,128)S(1)} %copy.12, f32[64,136]{0,1:T(8,128)S(1)} %get-tuple-element.7, f32[264,64]{0,1:T(8,128)S(1)} %copy.11, bf16[136]{0:T(256)(128)(2,1)S(1)} %and_convert_fusion, bf16[264]{0:T(512)(128)(2,1)S(1)} %fusion.28), kind=kLoop, calls=%fused_computation.22 | loop fusion | flops 16084992 | bytes 4801312 | tf_op jit(solution)/shard_map/max | solution.py:65
  249.1 0.0 copy-start.3
  249.1 22.0 %copy.14 = bf16[264,64,1,8,17]{1,3,4,0,2:T(8,128)(2,1)} copy(bf16[264,64,1,8,17]{0,1,4,3,2:T(8,128)(2,1)} %bitcast.22) | data formatting | bytes 9191424 | tf_op jit(solution)/shard_map/conv_general_dilated | solution.py:29
  271.1 5.6 %slice.36 = bf16[264,64,1,7,8]{1,3,4,0,2:T(8,128)(2,1)} slice(bf16[264,64,1,8,17]{1,3,4,0,2:T(8,128)(2,1)} %copy.14), slice={[0:264], [0:64], [0:1], [1:8], [0:8]} | slice | bytes 3784704 | tf_op jit(solution)/shard_map/conv_general_dilated | solution.py:29
  276.7 0.0 copy-done.3
  276.7 19.7 %broadcast_select_fusion = f32[256,8,17,128]{3,1,2,0:T(8,128)} fusion(pred[8,17]{0,1:T(8,128)(4,1)S(1)} %copy-done.3, bf16[264,64,1,7,8]{1,3,4,0,2:T(8,128)(2,1)} %slice.36, bf16[264,64,1,8,17]{1,3,4,0,2:T(8,128)(2,1)} %copy.14, bf16[64,64,3,3]{0,1,3,2:T(8,128)(2,1)S(1)} %bitcast.26, bf16[64,64,3,3]{0,1,3,2:T(8,128)(2,1)S(1)} %bitcast.27), kind=kOutput, calls=%fused_computation.16 | convolution fusion | flops 5158854656 | bytes 24461448 | tf_op jit(solution)/shard_map/conv_general_dilated | solution.py:29
  296.5 14.8 %copy.17 = f32[256,8,17,128]{3,0,2,1:T(8,128)} copy(f32[256,8,17,128]{3,1,2,0:T(8,128)} %broadcast_select_fusion) | data formatting | bytes 35651584 | tf_op jit(solution)/shard_map/conv_general_dilated | solution.py:29
  311.3 0.0 copy-start.2
  311.3 6.9 %slice_bitcast_fusion = f32[256,128,128]{1,0,2:T(8,128)S(1)} fusion(f32[256,1,136,128]{3,0,2,1:T(8,128)} %bitcast.21), kind=kLoop, calls=%fused_computation.7 | loop fusion | bytes 33554432 | tf_op jit(solution)/shard_map/squeeze | solution.py:29
  318.2 0.0 copy-done.2
  318.2 0.0 copy-start.1
  318.2 9.2 %fusion.4 = bf16[256,64,128]{1,0,2:T(8,128)(2,1)} fusion(f32[256,128,128]{1,0,2:T(8,128)S(1)} %slice_bitcast_fusion, f32[64,128]{0,1:T(8,128)S(1)} %slice.33, f32[256,64]{1,0:T(8,128)S(1)} %slice.32, f32[64,128]{0,1:T(8,128)S(1)} %slice.31, f32[256,64]{1,0:T(8,128)S(1)} %slice.30, f32[64]{0:T(128)S(1)} %copy-done.2, f32[64]{0:T(128)S(1)} %broadcast_multiply_fusion, ...), kind=kLoop, calls=%fused_computation.6 | loop fusion | flops 25165824 | bytes 21169408 | tf_op jit(solution)/shard_map/convert_element_type | solution.py:75
  327.5 11.5 %copy.18 = bf16[256,64,128]{2,1,0:T(8,128)(2,1)} copy(bf16[256,64,128]{1,0,2:T(8,128)(2,1)} %fusion.4) | data formatting | bytes 8388608 | tf_op jit(solution)/shard_map/convert_element_type | solution.py:75
  339.0 0.0 copy-done.1
  (6 shorter events, 0.1 us)
Async XLA Ops:
  6.5 0.7 copy-start
  6.5 147.5 %all-gather.6.cloned.1.call-start = ((), (), s32[]{:S(2)}) async-start(), calls=%async_computation.1 | async-start | bytes 4325376 | tf_op jit(solution)/shard_map/all_gather | solution.py:49
  8.8 232.2 %all-gather.4.cloned.1.call-start = ((), (), s32[]{:S(2)}) async-start(), calls=%async_computation | async-start | bytes 1114112 | tf_op jit(solution)/shard_map/all_gather | solution.py:50
  249.1 27.7 %copy-start.3 = (pred[8,17]{0,1:T(8,128)(4,1)S(1)}, pred[8,17]{0,1:T(8,128)(4,1)}, u32[]{:S(2)}) copy-start(pred[8,17]{0,1:T(8,128)(4,1)} %constant.40) | copy-start | bytes 412
  311.3 6.9 %copy-start.2 = (f32[64]{0:T(128)S(1)}, f32[64]{0:T(128)}, u32[]{:S(2)}) copy-start(f32[64]{0:T(128)} %param.9) | copy-start | bytes 772
  318.2 20.8 %copy-start.1 = (bf16[256,16]{0,1:T(8,128)(2,1)S(1)}, bf16[256,16]{0,1:T(8,128)(2,1)}, u32[]{:S(2)}) copy-start(bf16[256,16]{0,1:T(8,128)(2,1)} %param.5) | copy-start | bytes 24580
Sparse Core Ops, SparseCore 0:
  9.4 144.5 all-gather.5
  157.4 83.5 all-gather.3
